TPU v7x, 32 devices: a whole 2x2x4 slice. The times are simulated.
32 devices in a mesh: dp: 4 (over y, x), ctx: 8 (over z, core).
Axes of the slice: x: 2, y: 2, z: 4, core: 2. Of those that a mesh axis runs over, the one named last changes fastest.
Arguments:
- tokens: bfloat16 [4096, 2048], P('ctx', 'dp'), may hold values from -6 to 6
- input_gain: float32 [2048], replicated, may hold values from 0.1 to 1.9
- projections: bfloat16 [3, 2048, 1024], P(None, 'dp'), may hold values from -0.125 to 0.125
- head_gain: float32 [1024], P('dp'), may hold values from 0.1 to 1.9
Outputs:
- attended: bfloat16 [4096, 1024], P('ctx', 'dp')
All inputs are finite; a program needn't handle non-finite values.
Results may differ from a plain program's by a relative error of at most 0.0061.
Values may be sent and summed in bfloat16 or wider, within the bound.
No kernel may reach another device: no remote copies, remote signals or barrier semaphores. Data moves between devices by JAX's collectives and lax.ppermute only.
A program may use at most 64 MiB of HBM per device.

v0:
```python
import jax
import jax.numpy as jnp
from jax import lax
from jax.sharding import PartitionSpec as P

HEAD_DIM = 128
epsilon = 1e-05


def entering(value, axis, join, neutral):
    count, mine = (lax.axis_size(axis), lax.axis_index(axis))
    pieces = lax.all_gather(value, axis)
    subtotal = jnp.full_like(value, 0) + jnp.asarray(neutral, value.dtype)

    def turn(position, subtotal):
        longer = join(subtotal, pieces[position])
        return jnp.where(position < mine, longer, subtotal)

    return lax.fori_loop(0, count - 1, turn, subtotal)


def feature(inputs):
    return jnp.where(inputs > 0, inputs + 1.0, jnp.exp(jnp.minimum(inputs, 0.0)))


def activate(products):
    return jnp.concatenate([feature(products[:2]), products[2:]], axis=0).astype(jnp.bfloat16)


def combine(earlier, later):
    return earlier + later


def body(tokens, input_gain, projections, head_gain):
    whole = lax.all_gather(tokens, "dp", axis=1, tiled=True)
    inputs = whole.astype(jnp.float32)
    steps = inputs.shape[0]
    scale = lax.rsqrt(jnp.mean(inputs * inputs, axis=-1, keepdims=True) + epsilon)
    normed = (inputs * scale * input_gain).astype(jnp.bfloat16)
    width = head_gain.shape[0]
    mine = lax.all_to_all(projections, "dp", split_axis=2, concat_axis=1, tiled=True)
    products = jnp.einsum("td,pdc->ptc", normed, mine, preferred_element_type=jnp.float32)
    stacked = activate(products)
    heads = width // HEAD_DIM
    queries = stacked[0].reshape(steps, heads, HEAD_DIM)
    key_feats = stacked[1].reshape(steps, heads, HEAD_DIM)
    values = stacked[2].reshape(steps, heads, HEAD_DIM)
    local_state = jnp.einsum("the,thf->hef", key_feats, values, preferred_element_type=jnp.float32)
    prior = entering(local_state, "ctx", combine, jnp.zeros_like(local_state))
    prior_state = prior.astype(jnp.bfloat16)
    positions = jnp.arange(steps, dtype=jnp.int32)
    causal = positions[:, None] >= positions[None, :]
    scores = jnp.einsum("the,she->hts", queries, key_feats, preferred_element_type=jnp.float32)
    scores = jnp.where(causal[None], scores, 0.0).astype(jnp.bfloat16)
    inner = jnp.einsum("hts,shf->thf", scores, values, preferred_element_type=jnp.float32)
    outer = jnp.einsum("the,hef->thf", queries, prior_state, preferred_element_type=jnp.float32)
    mixed_out = inner + outer
    factor = lax.rsqrt(jnp.mean(mixed_out * mixed_out, axis=-1, keepdims=True) + epsilon)
    attended = mixed_out * factor * head_gain.reshape(heads, HEAD_DIM)
    return attended.astype(jnp.bfloat16).reshape(steps, width)


def solution(mesh):
    in_specs = (P("ctx", "dp"), P(), P(None, "dp", None), P("dp"))
    out_specs = P("ctx", "dp")
    return jax.shard_map(body, mesh=mesh, in_specs=in_specs, out_specs=out_specs, check_vma=False)
```

profile of v0, /device:TPU:0, one launch (start us, length us, event | category | flops | bytes accessed | tf_op | source)
XLA Modules:
  0.0 136.9 jit_solution(17386029378452002127)
XLA Ops:
  6.5 0.0 all-gather.4.cloned.1.call-start
  6.5 0.7 all-gather.4.cloned.1.call-update
  7.3 0.0 all-gather.6.cloned.1.call-start
  7.3 7.6 %copy.10 = bf16[3,512,1024]{1,0,2:T(4,128)(2,1)} copy(bf16[3,512,1024]{2,1,0:T(8,128)(2,1)} %param.8) | data formatting | bytes 6291456 | tf_op args[2]
  14.9 69.5 %all_to_all.18 = bf16[3,512,1024]{1,0,2:T(4,128)(2,1)S(1)} all-to-all(bf16[3,512,1024]{1,0,2:T(4,128)(2,1)} %copy.10), channel_id=1, replica_groups=mesh['dp'=4,'ctx'=8] {'dp'}, dimensions={2} | all-to-all | bytes 6291456 | tf_op jit(solution)/shard_map/all_to_all | solution.py:41
  84.4 3.0 %copy.20 = bf16[3,512,4,256]{1,2,3,0:T(4,128)(2,1)S(1)} copy(bf16[3,512,4,256]{1,0,3,2:T(4,128)(2,1)S(1)} %bitcast.32) | data formatting | bytes 6291456 | tf_op jit(solution)/shard_map/all_to_all | solution.py:41
  87.4 0.0 copy-start.1
  87.4 4.0 %all_to_all.16 = bf16[3,2048,256]{1,2,0:T(8,128)(2,1)} reshape(bf16[3,4,512,256]{2,1,3,0:T(4,128)(2,1)S(1)} %bitcast.33) | data formatting | bytes 6291456 | tf_op jit(solution)/shard_map/all_to_all | solution.py:41
  91.4 0.0 all-gather.4.cloned.1.call-done
  91.4 2.1 %fusion = f32[512]{0:T(512)S(1)} fusion(bf16[512,2048]{1,0:T(8,128)(2,1)} %all-gather.4.cloned.1.call-done), kind=kLoop, calls=%fused_computation.3 | loop fusion | flops 3145216 | bytes 2099200 | tf_op jit(solution)/shard_map/reduce_sum | solution.py:38
  93.5 0.0 copy-done.1
  93.5 4.4 %fusion.8 = f32[3,512,256]{1,2,0:T(8,128)S(1)} fusion(bf16[3,2048,256]{1,2,0:T(8,128)(2,1)} %all_to_all.16, bf16[512,2048]{1,0:T(8,128)(2,1)} %all-gather.4.cloned.1.call-done, f32[2048]{0:T(1024)S(1)} %copy-done.1, f32[512]{0:T(512)S(1)} %add_rsqrt_fusion.1), kind=kOutput, calls=%fused_computation.12 | convolution fusion | flops 1614807040 | bytes 6825984 | tf_op jit(solution)/shard_map/td,pdc->ptc/dot_general | solution.py:42
  97.9 0.2 select_convert_fusion.1
  98.2 0.9 fusion.20
  99.1 0.0 copy-start
  99.1 0.0 all-gather.6.cloned.1.call-update
  99.1 0.1 iota_compare_fusion
  99.2 22.0 %all-gather.6.cloned.1.call-done = f32[16,128,128]{2,1,0:T(8,128)} async-done(((f32[2,128,128]{2,1,0:T(8,128)}), f32[16,128,128]{2,1,0:T(8,128)}) %all-gather.6.cloned.1.call-update) | async-done | bytes 1048592 | tf_op jit(solution)/shard_map/all_gather | solution.py:12
  121.3 6.8 %while.14 = (s32[]{:T(128)}, f32[2,128,128]{2,1,0:T(8,128)S(1)}, s32[]{:T(128)}, f32[8,2,128,128]{3,2,1,0:T(8,128)}, s32[]{:T(128)}, /*index=5*/s32[]{:T(128)}) while((s32[]{:T(128)}, f32[2,128,128]{2,1,0:T(8,128)S(1)}, s32[]{:T(128)}, f32[8,2,128,128]{3,2,1,0:T(8,128)}, s32[]{:T(128)}, /*index=5*/s32[]{:T(128)}) %tuple.41), condition=%wide.region_2.3_spmd.clone, body=%wide.region_1.2_spmd.clone.sunk | while | flops 98308 | bytes 393317 | solution.py:19
  121.3 0.9 add_select_fusion.2
  122.2 0.9 add_select_fusion.2
  123.2 0.9 add_select_fusion.2
  124.2 0.9 add_select_fusion.2
  125.1 0.9 add_select_fusion.2
  126.1 0.9 add_select_fusion.2
  127.1 0.9 add_select_fusion.2
  128.1 0.3 fusion.16
  128.3 0.8 multiply_reduce_fusion
  129.1 0.0 copy-done
  129.2 0.1 multiply_convert_fusion
  129.3 0.8 copy.15
  (5 shorter events, 0.1 us)
Async XLA Ops:
  6.5 84.8 %all-gather.4.cloned.1.call-start = ((), (), s32[]{:S(2)}) async-start(), calls=%async_computation.1 | async-start | bytes 2621440 | tf_op jit(solution)/shard_map/all_gather | solution.py:35
  7.3 114.0 %all-gather.6.cloned.1.call-start = ((), (), s32[]{:S(2)}) async-start(), calls=%async_computation.2 | async-start | bytes 1179648 | tf_op jit(solution)/shard_map/all_gather | solution.py:12
  87.4 6.1 %copy-start.1 = (f32[2048]{0:T(1024)S(1)}, f32[2048]{0:T(1024)}, u32[]{:S(2)}) copy-start(f32[2048]{0:T(1024)} %param.7) | copy-start | bytes 24580
  99.1 30.0 %copy-start = (f32[256]{0:T(256)S(1)}, f32[256]{0:T(256)}, u32[]{:S(2)}) copy-start(f32[256]{0:T(256)} %param.9) | copy-start | bytes 3076
Sparse Core Ops, SparseCore 0:
  9.2 70.0 all-gather.3
  99.3 21.9 all-gather.5
where the time goes:
time: 137 us
  blocking collectives  69.5 us (51%)
  waiting for transfers between devices  22.7 us (17%)
  local copies, waits for them, and re-layouts  15.5 us (11%)
  between operations  13.5 us (10%)
  other arithmetic  9.16 us (7%)
  matrix products  6.37 us (5%)
    all_to_all x1, blocking collectives, body(): lax.all_to_all(projections, 'dp', split_axis=2, concat_axis=1, tiled=True)  69.5 us
    all_gather x1, waiting for transfers between devices, entering(): pieces = lax.all_gather(value, axis)  22 us
    unnamed x5, local copies, waits for them, and re-layouts  7.62 us
    all_to_all x2, local copies, waits for them, and re-layouts, body(): lax.all_to_all(projections, 'dp', split_axis=2, concat_axis=1, tiled=True)  6.93 us
    select_n x7, other arithmetic, turn(): return jnp.where(position < mine, longer, subtotal)  6.65 us
    dot_general x1, matrix products, body(): jnp.einsum('td,pdc->ptc', normed, mine, preferred_element_type=jnp.float32)  4.42 us
  transfers between devices with their start and end apart: 2, of which 1 were waited for; matrix products, arithmetic and copies ran while one was open for 8% of the time, Pallas kernels for 0%

commit v1 on v0

--- a/solution.py
+++ b/solution.py
@@ -38,7 +38,10 @@
     scale = lax.rsqrt(jnp.mean(inputs * inputs, axis=-1, keepdims=True) + epsilon)
     normed = (inputs * scale * input_gain).astype(jnp.bfloat16)
     width = head_gain.shape[0]
-    mine = lax.all_to_all(projections, "dp", split_axis=2, concat_axis=1, tiled=True)
+    mine = jnp.concatenate(
+        lax.all_to_all(jnp.stack(jnp.split(projections, lax.axis_size("dp"), axis=2)), "dp", 0, 0),
+        axis=1,
+    )
     products = jnp.einsum("td,pdc->ptc", normed, mine, preferred_element_type=jnp.float32)
     stacked = activate(products)
     heads = width // HEAD_DIM

time: 137 us -> 122 us (0.89)
  blocking collectives: 69.5 us -> 57.6 us
  local copies, waits for them, and re-layouts: 15.5 us -> 12.1 us
    all_to_all x1, blocking collectives: 69.5 us -> 57.6 us  [body(): lax.all_to_all(jnp.stack(jnp.split(projections, lax.axis_size('dp'), axis...]
    reshape x0 -> x2, local copies, waits for them, and re-layouts: none -> 9.09 us  [body(): jnp.concatenate(lax.all_to_all(jnp.stack(jnp.split(projections, lax.axis_...]
    unnamed x5 -> x4, local copies, waits for them, and re-layouts: 7.62 us -> 0.01 us
    all_to_all x2 -> x0, local copies, waits for them, and re-layouts: 6.93 us -> none  [body(): lax.all_to_all(projections, 'dp', split_axis=2, concat_axis=1, tiled=True)]
    another operation x0 -> x1, local copies, waits for them, and re-layouts: none -> 2.09 us  [body(): jnp.stack(jnp.split(projections, lax.axis_size('dp'), axis=2))]
  transfers between devices with their start and end apart: 2 -> 2, of which waited for: 1 -> 1; matrix products, arithmetic and copies ran while one was open for 8% -> 10% of each run, Pallas kernels for 0% -> 0%
where the time goes in v1:
time: 122 us
  blocking collectives  57.6 us (47%)
  waiting for transfers between devices  23.6 us (19%)
  between operations  13.5 us (11%)
  local copies, waits for them, and re-layouts  12.1 us (10%)
  other arithmetic  9.6 us (8%)
  matrix products  5.44 us (4%)
    all_to_all x1, blocking collectives, body(): lax.all_to_all(jnp.stack(jnp.split(projections, lax.axis_size('dp'), axis...  57.6 us
    all_gather x1, waiting for transfers between devices, entering(): pieces = lax.all_gather(value, axis)  22.8 us
    reshape x2, local copies, waits for them, and re-layouts, body(): jnp.concatenate(lax.all_to_all(jnp.stack(jnp.split(projections, lax.axis_...  9.09 us
    select_n x7, other arithmetic, turn(): return jnp.where(position < mine, longer, subtotal)  6.65 us
    dot_general x1, matrix products, body(): jnp.einsum('td,pdc->ptc', normed, mine, preferred_element_type=jnp.float32)  3.49 us
  transfers between devices with their start and end apart: 2, of which 1 were waited for; matrix products, arithmetic and copies ran while one was open for 10% of the time, Pallas kernels for 0%

profile of v1, /device:TPU:0, one launch (start us, length us, event | category | flops | bytes accessed | tf_op | source)
XLA Modules:
  0.0 122.0 jit_solution(5105363286985591891)
XLA Ops:
  6.5 0.0 all-gather.4.cloned.1.call-start
  6.5 0.7 all-gather.4.cloned.1.call-update
  7.3 0.0 all-gather.6.cloned.1.call-start
  7.3 2.1 %slice_bitcast_fusion.3 = (bf16[1,3,512,256]{3,2,1,0:T(8,128)(2,1)S(1)}, bf16[1,3,512,256]{3,2,1,0:T(8,128)(2,1)S(1)}, bf16[1,3,512,256]{3,2,1,0:T(8,128)(2,1)S(1)}, bf16[1,3,512,256]{3,2,1,0:T(8,128)(2,1)S(1)}) fusion(bf16[3,512,1024]{2,1,0:T(8,128)(2,1)} %param.8), kind=kLoop, calls=%fused_computation.23 | loop fusion | bytes 6291456 | tf_op jit(solution)/shard_map/stack | solution.py:42
  9.4 0.4 pad_maximum_fusion
  9.8 57.6 %all_to_all.5 = bf16[4,3,512,256]{3,2,1,0:T(8,128)(2,1)S(1)} all-to-all(bf16[4,3,512,256]{3,2,1,0:T(8,128)(2,1)S(1)} %pad_maximum_fusion), channel_id=1, replica_groups=mesh['dp'=4,'ctx'=8] {'dp'}, dimensions={0} | all-to-all | bytes 6291456 | tf_op jit(solution)/shard_map/all_to_all | solution.py:42
  67.4 4.4 %copy.10 = bf16[3,4,512,256]{2,1,3,0:T(4,128)(2,1)} copy(bf16[3,4,512,256]{3,2,0,1:T(8,128)(2,1)S(1)} %bitcast.37) | data formatting | bytes 6291456 | tf_op jit(solution)/shard_map/reshape | solution.py:41
  71.8 0.0 copy-start.1
  71.8 4.7 %reshape.40 = bf16[3,2048,256]{1,2,0:T(8,128)(2,1)S(1)} reshape(bf16[3,4,512,256]{2,1,3,0:T(4,128)(2,1)} %copy.10) | data formatting | bytes 6291456 | tf_op jit(solution)/shard_map/reshape | solution.py:41
  76.5 0.0 all-gather.4.cloned.1.call-done
  76.5 2.1 %fusion = f32[512]{0:T(512)S(1)} fusion(bf16[512,2048]{1,0:T(8,128)(2,1)} %all-gather.4.cloned.1.call-done), kind=kLoop, calls=%fused_computation.3 | loop fusion | flops 3145216 | bytes 2099200 | tf_op jit(solution)/shard_map/reduce_sum | solution.py:38
  78.6 0.0 copy-done.1
  78.6 3.5 %fusion.8 = f32[3,512,256]{1,2,0:T(8,128)S(1)} fusion(bf16[3,2048,256]{1,2,0:T(8,128)(2,1)S(1)} %reshape.40, bf16[512,2048]{1,0:T(8,128)(2,1)} %all-gather.4.cloned.1.call-done, f32[2048]{0:T(1024)S(1)} %copy-done.1, f32[512]{0:T(512)S(1)} %add_rsqrt_fusion.1), kind=kOutput, calls=%fused_computation.12 | convolution fusion | flops 1614807040 | bytes 6825984 | tf_op jit(solution)/shard_map/td,pdc->ptc/dot_general | solution.py:45
  82.1 0.2 select_convert_fusion.1
  82.4 0.9 fusion.20
  83.3 0.0 copy-start
  83.3 0.0 all-gather.6.cloned.1.call-update
  83.4 0.1 iota_compare_fusion
  83.5 22.8 %all-gather.6.cloned.1.call-done = f32[16,128,128]{2,1,0:T(8,128)} async-done(((f32[2,128,128]{2,1,0:T(8,128)}), f32[16,128,128]{2,1,0:T(8,128)}) %all-gather.6.cloned.1.call-update) | async-done | bytes 1048592 | tf_op jit(solution)/shard_map/all_gather | solution.py:12
  106.3 6.8 %while.14 = (s32[]{:T(128)}, f32[2,128,128]{2,1,0:T(8,128)S(1)}, s32[]{:T(128)}, f32[8,2,128,128]{3,2,1,0:T(8,128)}, s32[]{:T(128)}, /*index=5*/s32[]{:T(128)}) while((s32[]{:T(128)}, f32[2,128,128]{2,1,0:T(8,128)S(1)}, s32[]{:T(128)}, f32[8,2,128,128]{3,2,1,0:T(8,128)}, s32[]{:T(128)}, /*index=5*/s32[]{:T(128)}) %tuple.44), condition=%wide.region_2.3_spmd.clone, body=%wide.region_1.2_spmd.clone.sunk | while | flops 98308 | bytes 393309 | solution.py:19
  106.3 0.9 add_select_fusion.2
  107.3 0.9 add_select_fusion.2
  108.2 0.9 add_select_fusion.2
  109.2 0.9 add_select_fusion.2
  110.2 0.9 add_select_fusion.2
  111.2 0.9 add_select_fusion.2
  112.1 0.9 add_select_fusion.2
  113.1 0.3 fusion.16
  113.4 0.8 multiply_reduce_fusion
  114.2 0.0 copy-done
  114.2 0.1 multiply_convert_fusion
  114.3 0.8 copy.14
  (5 shorter events, 0.1 us)
Async XLA Ops:
  6.5 70.0 %all-gather.4.cloned.1.call-start = ((), (), s32[]{:S(2)}) async-start(), calls=%async_computation.1 | async-start | bytes 2621440 | tf_op jit(solution)/shard_map/all_gather | solution.py:35
  7.3 99.0 %all-gather.6.cloned.1.call-start = ((), (), s32[]{:S(2)}) async-start(), calls=%async_computation.2 | async-start | bytes 1179648 | tf_op jit(solution)/shard_map/all_gather | solution.py:12
  71.8 6.8 %copy-start.1 = (f32[2048]{0:T(1024)S(1)}, f32[2048]{0:T(1024)}, u32[]{:S(2)}) copy-start(f32[2048]{0:T(1024)} %param.7) | copy-start | bytes 24580
  83.3 30.8 %copy-start = (f32[256]{0:T(256)S(1)}, f32[256]{0:T(256)}, u32[]{:S(2)}) copy-start(f32[256]{0:T(256)} %param.9) | copy-start | bytes 3076
Sparse Core Ops, SparseCore 0:
  9.2 58.7 all-gather.3
  83.5 22.7 all-gather.5
